TPU v7x, 512 devices: a whole 4x8x8 slice. The times are simulated.
512 devices in a mesh: rep: 4 (over x), node: 16 (over y, core), local: 8 (over z).
Axes of the slice: x: 4, y: 8, z: 8, core: 2. Of those that a mesh axis runs over, the one named last changes fastest.
Arguments:
- tokens: bfloat16 [8192, 4096], P(('rep', 'node', 'local')), may hold values from -6 to 6
- expert_ids: int32 [8192, 8], P(('rep', 'node', 'local')), may hold values from 0 to 127, all different within a row; in each aligned block of 16 rows (0 to 15, 16 to 31, ...) at most 2 rows name the same one
- route_weights: float32 [8192, 8], P(('rep', 'node', 'local')), may hold values from 0.1 to 1
- gate_weight: bfloat16 [128, 768, 4096], P(('node', 'local'), 'rep'), may hold values from -0.09375 to 0.09375
- up_weight: bfloat16 [128, 768, 4096], P(('node', 'local'), 'rep'), may hold values from -0.09375 to 0.09375
- down_weight: bfloat16 [128, 768, 4096], P(('node', 'local'), None, 'rep'), may hold values from -0.21875 to 0.21875
Outputs:
- mixed_rows: bfloat16 [8192, 4096], P(('rep', 'node', 'local'))
Inputs may be any that keep to these rules, and one draw needn't show every extreme that they name: `expert_ids`: each row names 8 different experts. Among the rows of one device (aligned blocks of 16 rows) no expert is named by more than 2 rows, and in some blocks some expert is named by exactly 2 rows.
All inputs are finite; a program needn't handle non-finite values.
Results may differ from a plain program's by a relative error of at most 0.0057.
Values may be sent and summed in bfloat16 or wider, within the bound.
A program may use at most 64 MiB of HBM per device.

v0:
```python
import jax
import jax.numpy as jnp
from jax import lax
from jax.sharding import PartitionSpec as P


def slot_table(expert_ids, expert_count, slot_cap):
    row_count, top_count = expert_ids.shape
    flat_ids = expert_ids.reshape(-1)
    same = flat_ids[:, None] == flat_ids[None, :]
    place = jnp.arange(row_count * top_count, dtype=jnp.int32)
    rank_of = jnp.sum((same & (place[None, :] < place[:, None])).astype(jnp.int32), axis=1)
    return (flat_ids * slot_cap + rank_of).reshape(row_count, top_count)


def route_slots(blocks):
    return lax.all_to_all(blocks, ("node", "local"), split_axis=1, concat_axis=1, tiled=True)


def on_device(tokens, expert_ids, route_weights, gate_weight, up_weight, down_weight):
    row_count, top_count = expert_ids.shape
    model_width = tokens.shape[1]
    node_count = lax.axis_size("node")
    plane_count = lax.axis_size("rep")
    expert_count = node_count * lax.axis_size("local")
    slot_cap = min(row_count, max(2, 2 * row_count * top_count // expert_count))
    slot_total = expert_count * slot_cap
    slot_of = slot_table(expert_ids, expert_count, slot_cap)
    slot_iota = jnp.arange(slot_total, dtype=jnp.int32)
    placed = jnp.any(slot_of[None, :, :] == slot_iota[:, None, None], axis=2).astype(jnp.bfloat16)
    outgoing = jnp.dot(placed, tokens, preferred_element_type=jnp.float32).astype(jnp.bfloat16)
    mixing = jnp.sum(
        jnp.where(slot_of[:, :, None] == slot_iota[None, None, :], route_weights[:, :, None], 0.0),
        axis=1,
    )
    arrived = route_slots(outgoing.reshape(1, expert_count, slot_cap, model_width))
    arrived = arrived.reshape(slot_total, model_width)
    gate_local = gate_weight[0]
    up_local = up_weight[0]
    down_local = down_weight[0]
    quarter_width = down_local.shape[1]
    feature_dims = (((1,), (1,)), ((), ()))
    shard_piece = lax.all_gather(arrived, "rep", axis=0, tiled=True)
    gate_part = lax.dot_general(
        shard_piece, gate_local, feature_dims, preferred_element_type=jnp.float32
    )
    up_part = lax.dot_general(
        shard_piece, up_local, feature_dims, preferred_element_type=jnp.float32
    )
    hidden_part = (jax.nn.silu(gate_part) * up_part).astype(jnp.bfloat16)
    expert_out = jnp.dot(
        lax.all_gather(hidden_part, "rep", axis=1, tiled=True),
        down_local,
        preferred_element_type=jnp.float32,
    ).astype(jnp.bfloat16)
    own_slots = lax.all_to_all(
        expert_out.reshape(plane_count, slot_total, quarter_width),
        "rep",
        split_axis=0,
        concat_axis=2,
        tiled=True,
    )
    returned = route_slots(own_slots.reshape(1, expert_count, slot_cap, model_width))
    back_rows = returned.reshape(slot_total, model_width).astype(jnp.float32)
    mixed_rows = jnp.dot(mixing, back_rows, precision=lax.Precision.HIGHEST)
    return mixed_rows.astype(jnp.bfloat16)


def solution(mesh):
    placed = (
        P(("rep", "node", "local"), None),
        P(("rep", "node", "local"), None),
        P(("rep", "node", "local"), None),
        P(("node", "local"), "rep", None),
        P(("node", "local"), "rep", None),
        P(("node", "local"), None, "rep"),
    )
    return jax.shard_map(
        on_device,
        mesh=mesh,
        in_specs=placed,
        out_specs=P(("rep", "node", "local"), None),
        check_vma=False,
    )
```

profile of v0, /device:TPU:1, one launch (start us, length us, event | category | flops | bytes accessed | tf_op | source)
XLA Modules:
  0.0 339.2 jit_solution(8202762404922500141)
XLA Ops:
  6.5 0.0 copy-start
  6.5 0.0 all-gather.3.cloned.1.call-start
  6.5 0.9 copy.20
  7.4 0.1 eq.20
  7.5 0.2 convert_reduce_fusion
  7.7 0.1 reduce_sum.21
  7.8 0.1 fusion.11
  7.9 3.0 convolution_convert_fusion
  10.9 4.4 %reshape.32 = bf16[1,128,2,4096]{3,2,1,0:T(2,128)(2,1)} reshape(bf16[256,4096]{1,0:T(8,128)(2,1)} %convolution_convert_fusion) | data formatting | bytes 4194304 | tf_op jit(solution)/shard_map/reshape | solution.py:36
  15.3 72.7 %all_to_all.25 = bf16[1,128,2,4096]{3,2,0,1:T(2,128)(2,1)} all-to-all(bf16[1,128,2,4096]{3,2,0,1:T(2,128)(2,1)} %bitcast.31), channel_id=1, replica_groups=mesh['rep'=4,'node'=16,'local'=8] {'node','local'}, dimensions={1} | all-to-all | bytes 4194304 | tf_op jit(solution)/shard_map/all_to_all | solution.py:17
  88.0 4.1 %reshape.33 = bf16[256,4096]{1,0:T(8,128)(2,1)} reshape(bf16[1,128,2,4096]{3,2,0,1:T(2,128)(2,1)} %all_to_all.25) | data formatting | bytes 4194304 | tf_op jit(solution)/shard_map/reshape | solution.py:37
  92.1 0.0 copy-start.3
  92.1 0.0 all-gather.3.cloned.1.call-update
  92.1 0.0 all-gather.5.cloned.1.call-start
  92.2 81.1 %all-gather.3.cloned.1.call-done = bf16[1024,4096]{1,0:T(8,128)(2,1)} async-done(((bf16[256,4096]{1,0:T(8,128)(2,1)}), bf16[1024,4096]{1,0:T(8,128)(2,1)}) %all-gather.3.cloned.1.call-update) | async-done | bytes 8388624 | tf_op jit(solution)/shard_map/all_gather | solution.py:43
  173.3 0.0 copy-done.3
  173.3 0.0 copy-start.2
  173.3 0.0 copy-start.4
  173.3 6.4 %fusion.3 = f32[1024,192]{0,1:T(8,128)S(1)} fusion(bf16[1024,4096]{1,0:T(8,128)(2,1)} %all-gather.3.cloned.1.call-done, bf16[1,192,4096]{2,1,0:T(8,128)(2,1)S(1)} %copy-done.3), kind=kOutput, calls=%fused_computation.6 | convolution fusion | flops 1610612736 | bytes 10747904 | tf_op jit(solution)/shard_map/dot_general | solution.py:44
  179.7 0.0 copy-done.2
  179.7 0.0 copy-done.4
  179.8 3.7 %fusion.8 = bf16[1024,192]{0,1:T(8,128)(2,1)} fusion(bf16[1024,4096]{1,0:T(8,128)(2,1)S(1)} %copy-done.2, bf16[1,192,4096]{2,1,0:T(8,128)(2,1)S(1)} %copy-done.4, f32[1024,192]{0,1:T(8,128)S(1)} %fusion.3), kind=kOutput, calls=%fused_computation.9 | convolution fusion | flops 1611792384 | bytes 11141120 | tf_op jit(solution)/shard_map/dot_general | solution.py:47
  183.4 0.0 all-gather.5.cloned.1.call-update
  183.5 33.0 %all-gather.5.cloned.1.call-done = bf16[1024,768]{0,1:T(8,128)(2,1)} async-done(((bf16[1024,192]{0,1:T(8,128)(2,1)}), bf16[1024,768]{0,1:T(8,128)(2,1)}) %all-gather.5.cloned.1.call-update) | async-done | bytes 1572880 | tf_op jit(solution)/shard_map/all_gather | solution.py:52
  216.5 0.0 copy-done
  216.5 3.2 convolution_convert_fusion.2
  219.7 27.8 %all_to_all.26 = bf16[4,256,1024]{2,1,0:T(8,128)(2,1)S(1)} all-to-all(bf16[4,256,1024]{2,1,0:T(8,128)(2,1)S(1)} %bitcast.33), channel_id=1, replica_groups=mesh['rep'=4,'node'=16,'local'=8] {'rep'}, dimensions={0} | all-to-all | bytes 4194304 | tf_op jit(solution)/shard_map/all_to_all | solution.py:56
  247.5 2.9 copy.24
  250.5 4.4 %reshape.35 = bf16[1,128,2,4096]{3,2,1,0:T(2,128)(2,1)} reshape(bf16[1,256,4,1024]{3,2,1,0:T(4,128)(2,1)} %copy.24) | data formatting | bytes 4194304 | tf_op jit(solution)/shard_map/reshape | solution.py:63
  254.8 0.0 copy-start.1
  254.8 16.4 %all-to-all-start.2 = ((bf16[1,128,2,4096]{3,2,0,1:T(2,128)(2,1)}), bf16[1,128,2,4096]{3,2,0,1:T(2,128)(2,1)}, u32[]{:S(2)}, u32[]{:S(2)}) async-start(bf16[1,128,2,4096]{3,2,0,1:T(2,128)(2,1)} %bitcast.30), calls=%async_computation.2 | async-start | bytes 4194304 | tf_op jit(solution)/shard_map/all_to_all | solution.py:17
  271.2 0.0 copy-done.1
  271.2 0.1 copy.22
  271.3 0.1 select_reduce_fusion
  271.4 53.6 %all-to-all-done.2 = bf16[1,128,2,4096]{3,2,0,1:T(2,128)(2,1)} async-done(((bf16[1,128,2,4096]{3,2,0,1:T(2,128)(2,1)}), bf16[1,128,2,4096]{3,2,0,1:T(2,128)(2,1)}, u32[]{:S(2)}, u32[]{:S(2)}) %all-to-all-start.2) | async-done | bytes 2097184 | tf_op jit(solution)/shard_map/all_to_all | solution.py:17
  325.0 4.1 %reshape.36 = bf16[256,4096]{1,0:T(8,128)(2,1)} reshape(bf16[1,128,2,4096]{3,2,0,1:T(2,128)(2,1)} %all-to-all-done.2) | data formatting | bytes 4194304 | tf_op jit(solution)/shard_map/reshape | solution.py:64
  329.1 3.2 convolution_convert_fusion.1
  (1 shorter events, 0.0 us)
Async XLA Ops:
  6.5 210.0 %copy-start = (bf16[1,768,1024]{2,1,0:T(8,128)(2,1)S(1)}, bf16[1,768,1024]{2,1,0:T(8,128)(2,1)}, u32[]{:S(2)}) copy-start(bf16[1,768,1024]{2,1,0:T(8,128)(2,1)} %param.11) | copy-start | bytes 4718596
  6.5 166.8 %all-gather.3.cloned.1.call-start = ((), (), s32[]{:S(2)}) async-start(), calls=%async_computation.3 | async-start | bytes 10485760 | tf_op jit(solution)/shard_map/all_gather | solution.py:43
  92.1 81.2 %copy-start.3 = (bf16[1,192,4096]{2,1,0:T(8,128)(2,1)S(1)}, bf16[1,192,4096]{2,1,0:T(8,128)(2,1)}, u32[]{:S(2)}) copy-start(bf16[1,192,4096]{2,1,0:T(8,128)(2,1)} %param.9) | copy-start | bytes 4718596
  92.1 124.4 %all-gather.5.cloned.1.call-start = ((), (), s32[]{:S(2)}) async-start(), calls=%async_computation.4 | async-start | bytes 1966080 | tf_op jit(solution)/shard_map/all_gather | solution.py:52
  173.3 6.4 %copy-start.2 = (bf16[1024,4096]{1,0:T(8,128)(2,1)S(1)}, bf16[1024,4096]{1,0:T(8,128)(2,1)}, u32[]{:S(2)}) copy-start(bf16[1024,4096]{1,0:T(8,128)(2,1)} %all-gather.3.cloned.1.call-done) | copy-start | bytes 25165828
  173.3 6.4 %copy-start.4 = (bf16[1,192,4096]{2,1,0:T(8,128)(2,1)S(1)}, bf16[1,192,4096]{2,1,0:T(8,128)(2,1)}, u32[]{:S(2)}) copy-start(bf16[1,192,4096]{2,1,0:T(8,128)(2,1)} %param.10) | copy-start | bytes 4718596
  254.8 16.4 %copy-start.1 = (f32[16,8]{0,1:T(8,128)S(1)}, f32[16,8]{0,1:T(8,128)}, u32[]{:S(2)}) copy-start(f32[16,8]{0,1:T(8,128)} %param.8) | copy-start | bytes 1540
  254.8 70.2 %all-to-all-start.2 = ((bf16[1,128,2,4096]{3,2,0,1:T(2,128)(2,1)}), bf16[1,128,2,4096]{3,2,0,1:T(2,128)(2,1)}, u32[]{:S(2)}, u32[]{:S(2)}) async-start(bf16[1,128,2,4096]{3,2,0,1:T(2,128)(2,1)} %bitcast.30), calls=%async_computation.2 | async-start | bytes 4194304 | tf_op jit(solution)/shard_map/all_to_all | solution.py:17
Sparse Core Ops, SparseCore 0:
  92.3 80.9 all-gather.2
  183.6 32.8 all-gather.4
where the time goes:
time: 340 us; the launch traced here: 339 us
  waiting for transfers between devices  168 us (49%)
  blocking collectives  100 us (29%)
  local copies, waits for them, and re-layouts  21.1 us (6%)
  matrix products  19.5 us (6%)
  starting transfers between devices  16.4 us (5%)
  between operations  13.5 us (4%)
    all_gather x1, waiting for transfers between devices, on_device(): shard_piece = lax.all_gather(arrived, 'rep', axis=0, tiled=True)  81.1 us
    all_to_all x1, blocking collectives, route_slots(): lax.all_to_all(blocks, ('node', 'local'), split_axis=1, concat_axis=1, ti...  72.7 us
    all_to_all x1, waiting for transfers between devices, route_slots(): lax.all_to_all(blocks, ('node', 'local'), split_axis=1, concat_axis=1, ti...  53.6 us
    all_gather x1, waiting for transfers between devices, on_device(): lax.all_gather(hidden_part, 'rep', axis=1, tiled=True)  33 us
    all_to_all x1, blocking collectives, on_device(): lax.all_to_all(expert_out.reshape(plane_count, slot_total, quarter_width)...  27.8 us
    all_to_all x1, starting transfers between devices, route_slots(): lax.all_to_all(blocks, ('node', 'local'), split_axis=1, concat_axis=1, ti...  16.4 us
  transfers between devices with their start and end apart: 3, of which 3 were waited for; matrix products, arithmetic and copies ran while one was open for 0% of the time, Pallas kernels for 0%

commit v1 on v0

v1 whole, which is shorter than its diff:
```python
import functools

import jax
import jax.numpy as jnp
from jax import lax
from jax.experimental import pallas as pl
from jax.experimental.pallas import tpu as pltpu
from jax.sharding import PartitionSpec as P

MESH = pl.DeviceIdType.MESH
BF, F32 = jnp.bfloat16, jnp.float32
META = 128


def near_first(ring):
    order = [0]
    for step in range(1, ring // 2 + 1):
        order += [step] if 2 * step == ring else [step, ring - step]
    return order


def kernel(dims, tok_ref, meta_ref, gate_ref, up_ref, down_ref, out_ref, *scratch):
    planes, ring, block, top, width, hidden = dims
    (
        rows_all, outgoing, arrived, weights, down, psend, pown, precv, hid, outs,
        returned, mix_hi, mix_lo, zsend, zrecv, fin, cols,
        s_x, r_x, s_m, r_m, s_w, r_w, s_ag, r_ag, s_a, r_a, s_p, r_p, s_h, r_h,
        s_b, r_b, s_z, r_z, s_f, r_f, l_sem,
    ) = scratch
    quarter = hidden // planes
    rows = planes * block
    slots = planes * 2
    msgs = 2 * ring
    msg_rows = ring * slots
    order = near_first(ring)
    back = [order.index((ring - d) % ring) for d in order]

    r = lax.axis_index("rep")
    node = lax.axis_index("node")
    z = lax.axis_index("local")
    y, c = node // 2, node % 2

    def x_peer(step):
        return ((r + step) % planes, node, z)

    def along(step, role, core):
        yy = (y + step * (1 - role)) % ring
        zz = (z + step * role) % ring
        return (r, 2 * yy + core, zz)

    def remote(src, dst, send, recv, device):
        return pltpu.make_async_remote_copy(
            src_ref=src, dst_ref=dst, send_sem=send, recv_sem=recv,
            device_id=device, device_id_type=MESH,
        )

    barrier = pltpu.get_barrier_semaphore()
    partners = [x_peer(s) for s in range(1, planes)]
    partners += [(r, 2 * y + (c + 1) % 2, z)]
    for d in range(1, ring):
        for core in range(2):
            partners += [along(d, 0, core), along(d, 1, core)]
    for p in partners:
        pl.semaphore_signal(barrier, inc=1, device_id=p, device_id_type=MESH)
    pl.semaphore_wait(barrier, len(partners))

    def col(p):
        return pl.ds(pl.multiple_of(p * width, 128), width)

    def row16(p, n=block):
        return pl.ds(pl.multiple_of(p * n, 16), n)

    def x_copies(step):
        p = (r + step) % planes
        here = row16(r)
        return (
            remote(tok_ref.at[:, col(p)], rows_all.at[0, here, pl.ds(0, width)],
                   s_x.at[step], r_x.at[step], x_peer(step)),
            remote(meta_ref, rows_all.at[0, here, pl.ds(width, META)],
                   s_m.at[step], r_m.at[step], x_peer(step)),
        )

    for step in range(1, planes):
        for cp in x_copies(step):
            cp.start()
    own_tok = pltpu.make_async_copy(tok_ref.at[:, col(r)], rows_all.at[0, row16(r), pl.ds(0, width)], l_sem.at[0])
    own_meta = pltpu.make_async_copy(meta_ref, rows_all.at[0, row16(r), pl.ds(width, META)], l_sem.at[1])
    own_tok.start()
    own_meta.start()

    def w_copies(step):
        p = (r + step) % planes
        here = row16(r, quarter)
        return (
            remote(gate_ref.at[0, :, col(p)], weights.at[0, here, :], s_w.at[0, step], r_w.at[0, step], x_peer(step)),
            remote(up_ref.at[0, :, col(p)], weights.at[1, here, :], s_w.at[1, step], r_w.at[1, step], x_peer(step)),
        )

    for step in range(1, planes):
        for cp in w_copies(step):
            cp.start()
    own_gate = pltpu.make_async_copy(gate_ref.at[0, :, col(r)], weights.at[0, row16(r, quarter), :], l_sem.at[2])
    own_up = pltpu.make_async_copy(up_ref.at[0, :, col(r)], weights.at[1, row16(r, quarter), :], l_sem.at[3])
    own_down = pltpu.make_async_copy(down_ref.at[0], down, l_sem.at[4])
    own_gate.start()
    own_up.start()
    own_down.start()

    own_tok.wait()
    own_meta.wait()
    for step in range(1, planes):
        for cp in x_copies(step):
            cp.wait_recv()

    def ag_copy(d):
        return remote(rows_all.at[0], rows_all.at[d and ring - d], s_ag.at[d], r_ag.at[d], along(d, 1 - c, c))

    for d in order[1:]:
        ag_copy(d).start()

    lanes = msgs * 2 * slots
    shape = (2 * rows, lanes)
    t = lax.broadcasted_iota(jnp.int32, shape, 0)
    q = lax.broadcasted_iota(jnp.int32, shape, 1)
    j = q // (2 * slots)
    pos, dc = j // 2, j % 2
    d_of = jnp.where(pos % 2 == 1, (pos + 1) // 2, (ring - pos // 2) % ring)
    expert = (2 * ((y + d_of * (1 - c)) % ring) + (c + dc) % 2) * ring + (z + d_of * c) % ring
    expert = expert.astype(F32)
    same_block = (t // rows) == ((q // slots) % 2)
    slot_left = ((q % slots) - 2 * ((t // block) % planes)).astype(F32)
    a = lax.broadcasted_iota(jnp.int32, (2 * rows, 2 * rows), 0)
    b = lax.broadcasted_iota(jnp.int32, (2 * rows, 2 * rows), 1)
    earlier = jnp.where((b < a) & (a // block == b // block), 1.0, 0.0).astype(BF)

    for pair in range(ring // 2):
        for d in (2 * pair, 2 * pair + 1):
            if d:
                ag_copy((ring - d) % ring).wait_recv()
        both = rows_all[2 * pair:2 * pair + 2].reshape(2 * rows, width + META)
        meta = both[:, width:].astype(F32)
        hits = jnp.zeros(shape, F32)
        high = jnp.zeros(shape, F32)
        low = jnp.zeros(shape, F32)
        for k in range(top):
            named = (meta[:, k:k + 1] == expert) & same_block
            hits = jnp.where(named, 1.0, hits)
            high = jnp.where(named, meta[:, top + k:top + k + 1], high)
            low = jnp.where(named, meta[:, 2 * top + k:2 * top + k + 1], low)
        rank = jnp.dot(earlier, hits.astype(BF), preferred_element_type=F32)
        here = (hits > 0.0) & (rank == slot_left)
        mix_hi[pair] = jnp.where(here, high, 0.0).astype(BF)
        mix_lo[pair] = jnp.where(here, low, 0.0).astype(BF)
        placed = jnp.where(here, 1.0, 0.0).T.astype(BF)
        sent = jnp.dot(placed, both[:, :width], preferred_element_type=F32).astype(BF)
        outgoing[:, 2 * pair * slots:2 * (pair + 1) * slots, :] = sent.reshape(msgs, 2 * slots, width)

    def a_copy(i, dc):
        return remote(
            outgoing.at[2 * i + dc], arrived.at[2 * back[i] + c],
            s_a.at[2 * i + dc], r_a.at[2 * back[i] + c], along(order[i], c, (c + dc) % 2),
        )

    for i in range(ring):
        for dc in range(2):
            if i or dc:
                a_copy(i, dc).start()
    own_slots = pltpu.make_async_copy(outgoing.at[0], arrived.at[c], r_a.at[c])
    own_slots.start()

    def wait_in(buf, sem):
        pltpu.make_async_copy(buf, buf, sem).wait()

    def p_copy(k, step):
        p = (r + step) % planes
        return remote(psend.at[k, p], precv.at[k, step], s_p.at[k, step], r_p.at[k, step], x_peer(step))

    def h_copy(k, step):
        return remote(hid.at[k, r], hid.at[k, r], s_h.at[k, step], r_h.at[k, step], x_peer(step))

    def first(k):
        for m in range(planes):
            wait_in(arrived.at[planes * k + m], r_a.at[planes * k + m])
        x = arrived[planes * k:planes * (k + 1)].reshape(planes * msg_rows, width)
        for half in range(2):
            part = lax.dot_general(x, weights[half], (((1,), (1,)), ((), ())), preferred_element_type=F32)
            part = part.reshape(planes, msg_rows, hidden)
            pown[k, :, :, half * hidden:(half + 1) * hidden] = part
            psend[k, :, :, half * hidden:(half + 1) * hidden] = part.astype(BF)
        for step in range(1, planes):
            p_copy(k, step).start()

    def second(k):
        total = pown[k, r]
        for step in range(1, planes):
            p_copy(k, step).wait_recv()
            total = total + precv[k, step].astype(F32)
        g, u = total[:, :hidden], total[:, hidden:]
        hid[k, r] = (g / (1.0 + jnp.exp(-g)) * u).astype(BF)
        for step in range(1, planes):
            h_copy(k, step).start()

    def b_copy(m):
        i, s = m // 2, m % 2
        dc = (c + s) % 2
        return remote(
            outs.at[m], returned.at[2 * back[i] + dc], s_b.at[m], r_b.at[2 * back[i] + dc],
            along(order[i], s, s),
        )

    def third(k):
        for step in range(1, planes):
            p = (r + planes - step) % planes
            wait_in(hid.at[k, p], r_h.at[k, step])
        h = hid[k].reshape(planes * msg_rows, hidden)
        o = jnp.dot(h, down[...], preferred_element_type=F32).astype(BF)
        outs[planes * k:planes * (k + 1)] = o.reshape(planes, msg_rows, width)
        for m in range(planes * k, planes * (k + 1)):
            if m < 2:
                @pl.when(c != m)
                def _():
                    b_copy(m).start()

                @pl.when(c == m)
                def _():
                    pltpu.make_async_copy(outs.at[m], returned.at[0], r_b.at[0]).start()
            else:
                b_copy(m).start()

    own_gate.wait()
    own_up.wait()
    own_down.wait()
    for step in range(1, planes):
        for cp in w_copies(step):
            cp.wait_recv()
    chunks = msgs // planes
    for step in range(chunks + 2):
        if step < chunks:
            first(step)
        if 0 <= step - 1 < chunks:
            second(step - 1)
        if 0 <= step - 2 < chunks:
            third(step - 2)

    for jj in range(msgs):
        wait_in(returned.at[jj], r_b.at[jj])

    def z_copy(d):
        return remote(zsend.at[d], zrecv.at[(ring - d) % ring], s_z.at[d], r_z.at[d], along(d, 1 - c, c))

    for pair in range(ring // 2):
        got = returned[:, 2 * pair * slots:2 * (pair + 1) * slots, :].reshape(lanes, width)
        part = jnp.dot(mix_hi[pair], got, preferred_element_type=F32)
        part = part + jnp.dot(mix_lo[pair], got, preferred_element_type=F32)
        zsend[2 * pair:2 * pair + 2] = part.reshape(2, rows, width).astype(BF)
        for d in (2 * pair, 2 * pair + 1):
            if d:
                z_copy(d).start()

    total = zsend[0].astype(F32)
    for d in range(1, ring):
        z_copy(d).wait_recv()
        total = total + zrecv[(ring - d) % ring].astype(F32)
    fin[...] = total.astype(BF).reshape(planes, block, width)

    def f_copy(step):
        p = (r + step) % planes
        return remote(fin.at[p], cols.at[r], s_f.at[step], r_f.at[step], x_peer(step))

    for step in range(1, planes):
        f_copy(step).start()
    own_cols = pltpu.make_async_copy(fin.at[r], cols.at[r], l_sem.at[5])
    own_cols.start()
    own_cols.wait()
    for step in range(1, planes):
        p = (r + planes - step) % planes
        wait_in(cols.at[p], r_f.at[step])
    for p in range(planes):
        out_ref[:, p * width:(p + 1) * width] = cols[p]

    for step in range(1, planes):
        for cp in x_copies(step) + w_copies(step):
            cp.wait_send()
        f_copy(step).wait_send()
        for k in range(chunks):
            p_copy(k, step).wait_send()
            h_copy(k, step).wait_send()
    for d in range(1, ring):
        ag_copy(d).wait_send()
        z_copy(d).wait_send()
    for i in range(ring):
        for dc in range(2):
            if i or dc:
                a_copy(i, dc).wait_send()
    for m in range(msgs):
        if m < 2:
            @pl.when(c != m)
            def _():
                b_copy(m).wait_send()
        else:
            b_copy(m).wait_send()


def on_device(tokens, expert_ids, route_weights, gate_weight, up_weight, down_weight):
    block, top = expert_ids.shape
    planes = lax.axis_size("rep")
    ring = lax.axis_size("local")
    width = down_weight.shape[2]
    hidden = down_weight.shape[1]
    quarter = hidden // planes
    rows, slots, msgs = planes * block, planes * 2, 2 * ring
    msg_rows, chunks = ring * slots, 2 * ring // planes
    high = lax.reduce_precision(route_weights, exponent_bits=8, mantissa_bits=7)
    meta = jnp.concatenate(
        [expert_ids.astype(F32), high, route_weights - high, jnp.zeros((block, META - 3 * top), F32)], axis=1
    ).astype(BF)
    dma = pltpu.SemaphoreType.DMA
    return pl.pallas_call(
        functools.partial(kernel, (planes, ring, block, top, width, hidden)),
        out_shape=jax.ShapeDtypeStruct(tokens.shape, BF),
        in_specs=[pl.BlockSpec(memory_space=pltpu.VMEM)] * 2 + [pl.BlockSpec(memory_space=pl.ANY)] * 3,
        out_specs=pl.BlockSpec(memory_space=pltpu.VMEM),
        scratch_shapes=[
            pltpu.VMEM((ring, rows, width + META), BF),
            pltpu.VMEM((msgs, msg_rows, width), BF),
            pltpu.VMEM((msgs, msg_rows, width), BF),
            pltpu.VMEM((2, hidden, width), BF),
            pltpu.VMEM((hidden, width), BF),
            pltpu.VMEM((chunks, planes, msg_rows, 2 * hidden), BF),
            pltpu.VMEM((chunks, planes, msg_rows, 2 * hidden), F32),
            pltpu.VMEM((chunks, planes, msg_rows, 2 * hidden), BF),
            pltpu.VMEM((chunks, planes, msg_rows, hidden), BF),
            pltpu.VMEM((msgs, msg_rows, width), BF),
            pltpu.VMEM((msgs, msg_rows, width), BF),
            pltpu.VMEM((ring // 2, 2 * rows, msgs * 2 * slots), BF),
            pltpu.VMEM((ring // 2, 2 * rows, msgs * 2 * slots), BF),
            pltpu.VMEM((ring, rows, width), BF),
            pltpu.VMEM((ring, rows, width), BF),
            pltpu.VMEM((planes, block, width), BF),
            pltpu.VMEM((planes, block, width), BF),
        ]
        + [dma((planes,))] * 4
        + [dma((2, planes))] * 2
        + [dma((ring,))] * 2
        + [dma((msgs,))] * 2
        + [dma((chunks, planes))] * 4
        + [dma((msgs,))] * 2
        + [dma((ring,))] * 2
        + [dma((planes,))] * 2
        + [dma((6,))],
        compiler_params=pltpu.CompilerParams(
            collective_id=0, has_side_effects=True, vmem_limit_bytes=56 * 2**20
        ),
    )(tokens, meta, gate_weight, up_weight, down_weight)


def solution(mesh):
    placed = (
        P(("rep", "node", "local"), None),
        P(("rep", "node", "local"), None),
        P(("rep", "node", "local"), None),
        P(("node", "local"), "rep", None),
        P(("node", "local"), "rep", None),
        P(("node", "local"), None, "rep"),
    )
    return jax.shard_map(
        on_device,
        mesh=mesh,
        in_specs=placed,
        out_specs=P(("rep", "node", "local"), None),
        check_vma=False,
    )
```

time: 340 us -> 170 us (0.50)
  the two profiles are of different devices: /device:TPU:1 before, /device:TPU:8 now
where the time goes in v1:
time: 170 us
  Pallas kernels  165 us (97%)
  local copies, waits for them, and re-layouts  2.57 us (2%)
  other arithmetic  2.06 us (1%)
    pallas_call x1, Pallas kernels, on_device(): pl.pallas_call(functools.partial(kernel, (planes, ring, block, top, width...  165 us

profile of v1, /device:TPU:8, one launch (start us, length us, event | category | flops | bytes accessed | tf_op | source)
XLA Modules:
  0.0 170.0 jit_solution(14691458017717639703)
XLA Ops:
  0.0 0.1 pad.3.clone
  0.1 0.7 convert_element_type.4
  0.8 0.1 copy.10
  0.9 0.7 reduce_precision.3
  1.6 0.1 copy.11
  1.6 0.8 copy.12
  2.4 0.7 maximum_maximum_fusion.meta_ref
  3.1 165.4 %shard_map.64 = bf16[16,4096]{1,0:T(8,128)(2,1)} custom-call(bf16[16,4096]{1,0:T(8,128)(2,1)} %tok_ref.1, bf16[16,128]{1,0:T(8,128)(2,1)} %maximum_maximum_fusion.meta_ref, bf16[1,192,4096]{2,1,0:T(8,128)(2,1)} %gate_ref.1, bf16[1,192,4096]{2,1,0:T(8,128)(2,1)} %up_ref.1, bf16[1,768,1024]{2,1,0:T(8,128)(2,1)} %down_ref.1), custom_call_target="tpu_custom_call" | custom-call | tf_op jit(solution)/shard_map/pallas_call | solution.py:318
  168.4 1.6 copy.15
  (2 shorter events, 0.0 us)

commit v2 on v1

v2 whole, which is shorter than its diff:
```python
import functools

import jax
import jax.numpy as jnp
from jax import lax
from jax.experimental import pallas as pl
from jax.experimental.pallas import tpu as pltpu
from jax.sharding import PartitionSpec as P

MESH = pl.DeviceIdType.MESH
BF, F32 = jnp.bfloat16, jnp.float32
META = 128


def near_first(ring):
    order = [0]
    for step in range(1, ring // 2 + 1):
        order += [step] if 2 * step == ring else [step, ring - step]
    return order


def kernel(dims, tok_ref, ids_ref, share_ref, gate_ref, up_ref, down_ref, out_ref, *scratch):
    planes, ring, block, top, width, hidden = dims
    (
        meta_ref, rows_all, outgoing, arrived, weights, down, psend, pown, precv, hid, outs,
        returned, mix_hi, mix_lo, zsend, zrecv, fin, cols,
        s_x, r_x, s_m, r_m, s_w, r_w, s_ag, r_ag, s_a, r_a, s_p, r_p, s_h, r_h,
        s_b, r_b, s_z, r_z, s_f, r_f, l_sem,
    ) = scratch
    quarter = hidden // planes
    rows = planes * block
    slots = planes * 2
    msgs = 2 * ring
    group = 2 * slots
    chunks = ring // 2
    part_rows = msgs * group // planes
    order = near_first(ring)
    back = [order.index((ring - d) % ring) for d in order]

    r = lax.axis_index("rep")
    node = lax.axis_index("node")
    z = lax.axis_index("local")
    y, c = node // 2, node % 2

    def x_peer(step):
        return ((r + step) % planes, node, z)

    def along(step, role, core):
        yy = (y + step * (1 - role)) % ring
        zz = (z + step * role) % ring
        return (r, 2 * yy + core, zz)

    def remote(src, dst, send, recv, device):
        return pltpu.make_async_remote_copy(
            src_ref=src, dst_ref=dst, send_sem=send, recv_sem=recv,
            device_id=device, device_id_type=MESH,
        )

    def col(p):
        return pl.ds(pl.multiple_of(p * width, 128), width)

    def row16(p, n=block):
        return pl.ds(pl.multiple_of(p * n, 16), n)

    barrier = pltpu.get_barrier_semaphore()
    partners = [x_peer(s) for s in range(1, planes)]
    partners += [(r, 2 * y + (c + 1) % 2, z)]
    for d in range(1, ring):
        for core in range(2):
            partners += [along(d, 0, core), along(d, 1, core)]
    for p in partners:
        pl.semaphore_signal(barrier, inc=1, device_id=p, device_id_type=MESH)

    own = [
        pltpu.make_async_copy(tok_ref.at[:, col(r)], rows_all.at[0, row16(r), pl.ds(0, width)], l_sem.at[0]),
        pltpu.make_async_copy(gate_ref.at[0, :, col(r)], weights.at[0, row16(r, quarter), :], l_sem.at[2]),
        pltpu.make_async_copy(up_ref.at[0, :, col(r)], weights.at[1, row16(r, quarter), :], l_sem.at[3]),
        pltpu.make_async_copy(down_ref.at[0], down, l_sem.at[4]),
    ]
    for cp in own:
        cp.start()

    share = share_ref[...]
    high = share.astype(BF)
    low = (share - high.astype(F32)).astype(BF)
    k_of = lax.broadcasted_iota(jnp.int32, (top, META), 0)
    l_of = lax.broadcasted_iota(jnp.int32, (top, META), 1)
    meta_own = jnp.zeros((block, META), F32)
    for n, part in enumerate((ids_ref[...].astype(F32).astype(BF), high, low)):
        pick = jnp.where(l_of == k_of + n * top, 1.0, 0.0).astype(BF)
        meta_own += lax.dot_general(part, pick, (((0,), (0,)), ((), ())), preferred_element_type=F32)
    meta_ref[...] = meta_own.astype(BF)
    own_meta = pltpu.make_async_copy(meta_ref, rows_all.at[0, row16(r), pl.ds(width, META)], l_sem.at[1])
    own_meta.start()
    pl.semaphore_wait(barrier, len(partners))

    def x_copies(step):
        p = (r + step) % planes
        here = row16(r)
        return (
            remote(tok_ref.at[:, col(p)], rows_all.at[0, here, pl.ds(0, width)],
                   s_x.at[step], r_x.at[step], x_peer(step)),
            remote(meta_ref, rows_all.at[0, here, pl.ds(width, META)],
                   s_m.at[step], r_m.at[step], x_peer(step)),
        )

    for step in range(1, planes):
        for cp in x_copies(step):
            cp.start()
    own[0].wait()
    own_meta.wait()
    for step in range(1, planes):
        for cp in x_copies(step):
            cp.wait_recv()

    def ag_copy(i):
        return remote(rows_all.at[0], rows_all.at[back[i]], s_ag.at[i], r_ag.at[back[i]], along(order[i], 1 - c, c))

    for i in range(1, ring):
        ag_copy(i).start()

    def w_copies(step):
        p = (r + step) % planes
        here = row16(r, quarter)
        return (
            remote(gate_ref.at[0, :, col(p)], weights.at[0, here, :], s_w.at[0, step], r_w.at[0, step], x_peer(step)),
            remote(up_ref.at[0, :, col(p)], weights.at[1, here, :], s_w.at[1, step], r_w.at[1, step], x_peer(step)),
        )

    for step in range(1, planes):
        for cp in w_copies(step):
            cp.start()

    lanes = msgs * group
    shape = (2 * rows, lanes)
    t = lax.broadcasted_iota(jnp.int32, shape, 0)
    q = lax.broadcasted_iota(jnp.int32, shape, 1)
    j = q // group
    pos, dc = j // 2, j % 2
    d_of = jnp.where(pos % 2 == 1, (pos + 1) // 2, (ring - pos // 2) % ring)
    expert = (2 * ((y + d_of * (1 - c)) % ring) + (c + dc) % 2) * ring + (z + d_of * c) % ring
    expert = expert.astype(F32)
    same_block = (t // rows) == ((q // slots) % 2)
    expert = jnp.where(same_block, expert, -1.0)
    slot_left = ((q % slots) - 2 * ((t // block) % planes)).astype(F32)
    a = lax.broadcasted_iota(jnp.int32, (2 * rows, 2 * rows), 0)
    b = lax.broadcasted_iota(jnp.int32, (2 * rows, 2 * rows), 1)
    earlier = jnp.where((b < a) & (a // block == b // block), 1.0, 0.0).astype(BF)

    def a_copy(k, i, dc):
        return remote(
            outgoing.at[k, 2 * i + dc], arrived.at[k, 2 * back[i] + c],
            s_a.at[k, 2 * i + dc], r_a.at[k, 2 * back[i] + c], along(order[i], c, (c + dc) % 2),
        )

    def own_slots(k):
        return pltpu.make_async_copy(outgoing.at[k, 0], arrived.at[k, c], r_a.at[k, c])

    def place(k):
        for i in (2 * k, 2 * k + 1):
            if i:
                remote(rows_all.at[0], rows_all.at[i], s_ag.at[i], r_ag.at[i], x_peer(1)).wait_recv()
        both = rows_all[2 * k:2 * k + 2].reshape(2 * rows, width + META)
        meta = both[:, width:].astype(F32)
        hits = jnp.zeros(shape, F32)
        high = jnp.zeros(shape, F32)
        low = jnp.zeros(shape, F32)
        for n in range(top):
            named = meta[:, n:n + 1] == expert
            hits = jnp.where(named, 1.0, hits)
            high = jnp.where(named, meta[:, top + n:top + n + 1], high)
            low = jnp.where(named, meta[:, 2 * top + n:2 * top + n + 1], low)
        rank = jnp.dot(earlier, hits.astype(BF), preferred_element_type=F32)
        here = (hits > 0.0) & (rank == slot_left)
        mix_hi[k] = jnp.where(here, high, 0.0).astype(BF)
        mix_lo[k] = jnp.where(here, low, 0.0).astype(BF)
        placed = jnp.where(here, 1.0, 0.0).T.astype(BF)
        sent = jnp.dot(placed, both[:, :width], preferred_element_type=F32).astype(BF)
        outgoing[k] = sent.reshape(msgs, group, width)
        for i in range(ring):
            for dc in range(2):
                if i or dc:
                    a_copy(k, i, dc).start()
        own_slots(k).start()

    def wait_in(buf, sem):
        pltpu.make_async_copy(buf, buf, sem).wait()

    def p_copy(k, step):
        p = (r + step) % planes
        return remote(psend.at[k, p], precv.at[k, step], s_p.at[k, step], r_p.at[k, step], x_peer(step))

    def h_copy(k, step):
        return remote(hid.at[k, r], hid.at[k, r], s_h.at[k, step], r_h.at[k, step], x_peer(step))

    def first(k):
        for m in range(msgs):
            wait_in(arrived.at[k, m], r_a.at[k, m])
        x = arrived[k].reshape(msgs * group, width)
        for half in range(2):
            part = lax.dot_general(x, weights[half], (((1,), (1,)), ((), ())), preferred_element_type=F32)
            part = part.reshape(planes, part_rows, hidden)
            pown[k, :, :, half * hidden:(half + 1) * hidden] = part
            psend[k, :, :, half * hidden:(half + 1) * hidden] = part.astype(BF)
        for step in range(1, planes):
            p_copy(k, step).start()

    def second(k):
        total = pown[k, r]
        for step in range(1, planes):
            p_copy(k, step).wait_recv()
            total = total + precv[k, step].astype(F32)
        g, u = total[:, :hidden], total[:, hidden:]
        hid[k, r] = (g / (1.0 + jnp.exp(-g)) * u).astype(BF)
        for step in range(1, planes):
            h_copy(k, step).start()

    def b_copy(k, m):
        i, s = m // 2, m % 2
        dc = (c + s) % 2
        return remote(
            outs.at[k, m], returned.at[k, 2 * back[i] + dc], s_b.at[k, m], r_b.at[k, 2 * back[i] + dc],
            along(order[i], s, s),
        )

    def third(k):
        for step in range(1, planes):
            p = (r + planes - step) % planes
            wait_in(hid.at[k, p], r_h.at[k, step])
        h = hid[k].reshape(msgs * group, hidden)
        o = jnp.dot(h, down[...], preferred_element_type=F32).astype(BF)
        outs[k] = o.reshape(msgs, group, width)
        for m in range(msgs):
            if m < 2:
                @pl.when(c != m)
                def _():
                    b_copy(k, m).start()

                @pl.when(c == m)
                def _():
                    pltpu.make_async_copy(outs.at[k, m], returned.at[k, 0], r_b.at[k, 0]).start()
            else:
                b_copy(k, m).start()

    def z_copy(i):
        return remote(zsend.at[i], zrecv.at[back[i]], s_z.at[i], r_z.at[back[i]], along(order[i], 1 - c, c))

    def mix(k):
        for jj in range(msgs):
            wait_in(returned.at[k, jj], r_b.at[k, jj])
        got = returned[k].reshape(lanes, width)
        part = jnp.dot(mix_hi[k], got, preferred_element_type=F32)
        part = part + jnp.dot(mix_lo[k], got, preferred_element_type=F32)
        zsend[2 * k:2 * k + 2] = part.reshape(2, rows, width).astype(BF)
        for i in (2 * k, 2 * k + 1):
            if i:
                z_copy(i).start()

    for k in range(chunks):
        place(k)
    for cp in own[1:]:
        cp.wait()
    for step in range(1, planes):
        for cp in w_copies(step):
            cp.wait_recv()
    stages = []
    for k in range(chunks):
        stages += [(2 * k, 0, first, k), (2 * k + 3, 1, second, k), (2 * k + 6, 2, third, k), (2 * k + 9, 3, mix, k)]
    for _, _, stage, k in sorted(stages, key=lambda e: e[:2]):
        stage(k)

    total = zsend[0].astype(F32)
    for i in range(1, ring):
        wait_in(zrecv.at[i], r_z.at[i])
        total = total + zrecv[i].astype(F32)
    fin[...] = total.astype(BF).reshape(planes, block, width)

    def f_copy(step):
        p = (r + step) % planes
        return remote(fin.at[p], cols.at[r], s_f.at[step], r_f.at[step], x_peer(step))

    for step in range(1, planes):
        f_copy(step).start()
    own_cols = pltpu.make_async_copy(fin.at[r], cols.at[r], l_sem.at[5])
    own_cols.start()

    for step in range(1, planes):
        for cp in x_copies(step) + w_copies(step):
            cp.wait_send()
        for k in range(chunks):
            p_copy(k, step).wait_send()
            h_copy(k, step).wait_send()
    for i in range(1, ring):
        ag_copy(i).wait_send()
        z_copy(i).wait_send()
    for k in range(chunks):
        for i in range(ring):
            for dc in range(2):
                if i or dc:
                    a_copy(k, i, dc).wait_send()
        for m in range(msgs):
            if m < 2:
                @pl.when(c != m)
                def _():
                    b_copy(k, m).wait_send()
            else:
                b_copy(k, m).wait_send()

    own_cols.wait()
    for step in range(1, planes):
        wait_in(cols.at[(r + planes - step) % planes], r_f.at[step])
    for p in range(planes):
        out_ref[:, p * width:(p + 1) * width] = cols[p]
    for step in range(1, planes):
        f_copy(step).wait_send()


def on_device(tokens, expert_ids, route_weights, gate_weight, up_weight, down_weight):
    block, top = expert_ids.shape
    planes = lax.axis_size("rep")
    ring = lax.axis_size("local")
    width = down_weight.shape[2]
    hidden = down_weight.shape[1]
    rows, group, msgs = planes * block, planes * 4, 2 * ring
    chunks = ring // 2
    part_rows = msgs * group // planes
    dma = pltpu.SemaphoreType.DMA
    return pl.pallas_call(
        functools.partial(kernel, (planes, ring, block, top, width, hidden)),
        out_shape=jax.ShapeDtypeStruct(tokens.shape, BF),
        in_specs=[pl.BlockSpec(memory_space=pltpu.VMEM)] * 3 + [pl.BlockSpec(memory_space=pl.ANY)] * 3,
        out_specs=pl.BlockSpec(memory_space=pltpu.VMEM),
        scratch_shapes=[
            pltpu.VMEM((block, META), BF),
            pltpu.VMEM((ring, rows, width + META), BF),
            pltpu.VMEM((chunks, msgs, group, width), BF),
            pltpu.VMEM((chunks, msgs, group, width), BF),
            pltpu.VMEM((2, hidden, width), BF),
            pltpu.VMEM((hidden, width), BF),
            pltpu.VMEM((chunks, planes, part_rows, 2 * hidden), BF),
            pltpu.VMEM((chunks, planes, part_rows, 2 * hidden), F32),
            pltpu.VMEM((chunks, planes, part_rows, 2 * hidden), BF),
            pltpu.VMEM((chunks, planes, part_rows, hidden), BF),
            pltpu.VMEM((chunks, msgs, group, width), BF),
            pltpu.VMEM((chunks, msgs, group, width), BF),
            pltpu.VMEM((chunks, 2 * rows, msgs * group), BF),
            pltpu.VMEM((chunks, 2 * rows, msgs * group), BF),
            pltpu.VMEM((ring, rows, width), BF),
            pltpu.VMEM((ring, rows, width), BF),
            pltpu.VMEM((planes, block, width), BF),
            pltpu.VMEM((planes, block, width), BF),
        ]
        + [dma((planes,))] * 4
        + [dma((2, planes))] * 2
        + [dma((ring,))] * 2
        + [dma((chunks, msgs))] * 2
        + [dma((chunks, planes))] * 4
        + [dma((chunks, msgs))] * 2
        + [dma((ring,))] * 2
        + [dma((planes,))] * 2
        + [dma((6,))],
        compiler_params=pltpu.CompilerParams(
            collective_id=0, has_side_effects=True, vmem_limit_bytes=56 * 2**20
        ),
    )(tokens, expert_ids.T, route_weights.T, gate_weight, up_weight, down_weight)


def solution(mesh):
    placed = (
        P(("rep", "node", "local"), None),
        P(("rep", "node", "local"), None),
        P(("rep", "node", "local"), None),
        P(("node", "local"), "rep", None),
        P(("node", "local"), "rep", None),
        P(("node", "local"), None, "rep"),
    )
    return jax.shard_map(
        on_device,
        mesh=mesh,
        in_specs=placed,
        out_specs=P(("rep", "node", "local"), None),
        check_vma=False,
    )
```

time: 170 us -> 143 us (0.84)
  the two profiles are of different devices: /device:TPU:8 before, /device:TPU:4 now
where the time goes in v2:
time: 143 us
  Pallas kernels  142 us (99%)
  local copies, waits for them, and re-layouts  1.57 us (1%)
    pallas_call x1, Pallas kernels, on_device(): pl.pallas_call(functools.partial(kernel, (planes, ring, block, top, width...  142 us

profile of v2, /device:TPU:4, one launch (start us, length us, event | category | flops | bytes accessed | tf_op | source)
XLA Modules:
  0.0 143.1 jit_solution(11046990862560940004)
XLA Ops:
  0.0 141.5 %shard_map.64 = bf16[16,4096]{1,0:T(8,128)(2,1)} custom-call(bf16[16,4096]{1,0:T(8,128)(2,1)} %tok_ref.1, s32[8,16]{1,0:T(8,128)} %bitcast.2, f32[8,16]{1,0:T(8,128)} %bitcast.3, bf16[1,192,4096]{2,1,0:T(8,128)(2,1)} %gate_ref.1, bf16[1,192,4096]{2,1,0:T(8,128)(2,1)} %up_ref.1, bf16[1,768,1024]{2,1,0:T(8,128)(2,1)} %down_ref.1), custom_call_target="tpu_custom_call" | custom-call | tf_op jit(solution)/shard_map/pallas_call | solution.py:328
  141.5 1.6 %copy.8 = bf16[16,4096]{1,0:T(8,128)(2,1)} copy(bf16[16,4096]{1,0:T(8,128)(2,1)} %shard_map.64) | data formatting | bytes 262144

commit v3 on v2

--- a/solution.py
+++ b/solution.py
@@ -22,9 +22,9 @@
 def kernel(dims, tok_ref, ids_ref, share_ref, gate_ref, up_ref, down_ref, out_ref, *scratch):
     planes, ring, block, top, width, hidden = dims
     (
-        meta_ref, rows_all, outgoing, arrived, weights, down, psend, pown, precv, hid, outs,
+        meta_ref, rows_all, outgoing, arrived, weights, down, psend, pown, precv, fwd, frecv, hid, outs,
         returned, mix_hi, mix_lo, zsend, zrecv, fin, cols,
-        s_x, r_x, s_m, r_m, s_w, r_w, s_ag, r_ag, s_a, r_a, s_p, r_p, s_h, r_h,
+        s_x, r_x, s_m, r_m, s_w, r_w, s_ag, r_ag, s_a, r_a, s_p, r_p, s_q, r_q, s_h, r_h, s_g, r_g,
         s_b, r_b, s_z, r_z, s_f, r_f, l_sem,
     ) = scratch
     quarter = hidden // planes
@@ -186,12 +186,25 @@
     def wait_in(buf, sem):
         pltpu.make_async_copy(buf, buf, sem).wait()
 
-    def p_copy(k, step):
-        p = (r + step) % planes
-        return remote(psend.at[k, p], precv.at[k, step], s_p.at[k, step], r_p.at[k, step], x_peer(step))
-
-    def h_copy(k, step):
-        return remote(hid.at[k, r], hid.at[k, r], s_h.at[k, step], r_h.at[k, step], x_peer(step))
+    near = (r + 1 - 2 * (r % 2), planes - 1 - r)
+    far = (r + 2) % planes
+
+    def plane(p):
+        return (p, node, z)
+
+    def p_copy(k, half, n):
+        to = near[half]
+        return remote(psend.at[k, half, far if n else to], precv.at[k, half, n], s_p.at[k, half, n], r_p.at[k, half, n], plane(to))
+
+    def q_copy(k, half):
+        return remote(fwd.at[k, half], frecv.at[k, half], s_q.at[k, half], r_q.at[k, half], plane(near[1 - half]))
+
+    def h_copy(k, n):
+        return remote(hid.at[k, r], hid.at[k, r], s_h.at[k, n], r_h.at[k, n], plane(near[n]))
+
+    def g_copy(k, n):
+        part = hid.at[k, near[n], :, pl.ds(n * (hidden // 2), hidden // 2)]
+        return remote(part, part, s_g.at[k, n], r_g.at[k, n], plane(near[1 - n]))
 
     def first(k):
         for m in range(msgs):
@@ -200,20 +213,32 @@
         for half in range(2):
             part = lax.dot_general(x, weights[half], (((1,), (1,)), ((), ())), preferred_element_type=F32)
             part = part.reshape(planes, part_rows, hidden)
-            pown[k, :, :, half * hidden:(half + 1) * hidden] = part
-            psend[k, :, :, half * hidden:(half + 1) * hidden] = part.astype(BF)
-        for step in range(1, planes):
-            p_copy(k, step).start()
+            pown[k, half] = part
+            psend[k, half] = part.astype(BF)
+            for n in (1, 0):
+                p_copy(k, half, n).start()
+
+    def pass_on(k):
+        for half in range(2):
+            p_copy(k, half, 1).wait_recv()
+            fwd[k, half] = (pown[k, half, near[1 - half]] + precv[k, half, 1].astype(F32)).astype(BF)
+            q_copy(k, half).start()
 
     def second(k):
-        total = pown[k, r]
-        for step in range(1, planes):
-            p_copy(k, step).wait_recv()
-            total = total + precv[k, step].astype(F32)
-        g, u = total[:, :hidden], total[:, hidden:]
+        sums = []
+        for half in range(2):
+            p_copy(k, half, 0).wait_recv()
+            q_copy(k, half).wait_recv()
+            sums.append(pown[k, half, r] + precv[k, half, 0].astype(F32) + frecv[k, half].astype(F32))
+        g, u = sums
         hid[k, r] = (g / (1.0 + jnp.exp(-g)) * u).astype(BF)
-        for step in range(1, planes):
-            h_copy(k, step).start()
+        for n in range(2):
+            h_copy(k, n).start()
+
+    def relay(k):
+        for n in range(2):
+            wait_in(hid.at[k, near[n]], r_h.at[k, n])
+            g_copy(k, n).start()
 
     def b_copy(k, m):
         i, s = m // 2, m % 2
@@ -224,9 +249,8 @@
         )
 
     def third(k):
-        for step in range(1, planes):
-            p = (r + planes - step) % planes
-            wait_in(hid.at[k, p], r_h.at[k, step])
+        for n in range(2):
+            wait_in(hid.at[k, far, :, pl.ds(n * (hidden // 2), hidden // 2)], r_g.at[k, n])
         h = hid[k].reshape(msgs * group, hidden)
         o = jnp.dot(h, down[...], preferred_element_type=F32).astype(BF)
         outs[k] = o.reshape(msgs, group, width)
@@ -264,8 +288,9 @@
         for cp in w_copies(step):
             cp.wait_recv()
     stages = []
-    for k in range(chunks):
-        stages += [(2 * k, 0, first, k), (2 * k + 3, 1, second, k), (2 * k + 6, 2, third, k), (2 * k + 9, 3, mix, k)]
+    for n, k in enumerate([*range(1, chunks), 0]):
+        for depth, (late, stage) in enumerate(((0, first), (4, pass_on), (7, second), (10, relay), (13, third), (17, mix))):
+            stages.append((3 * n + late, -depth, stage, k))
     for _, _, stage, k in sorted(stages, key=lambda e: e[:2]):
         stage(k)
 
@@ -287,13 +312,16 @@
     for step in range(1, planes):
         for cp in x_copies(step) + w_copies(step):
             cp.wait_send()
-        for k in range(chunks):
-            p_copy(k, step).wait_send()
-            h_copy(k, step).wait_send()
     for i in range(1, ring):
         ag_copy(i).wait_send()
         z_copy(i).wait_send()
     for k in range(chunks):
+        for n in range(2):
+            p_copy(k, n, 0).wait_send()
+            p_copy(k, n, 1).wait_send()
+            q_copy(k, n).wait_send()
+            h_copy(k, n).wait_send()
+            g_copy(k, n).wait_send()
         for i in range(ring):
             for dc in range(2):
                 if i or dc:
@@ -337,9 +365,11 @@
             pltpu.VMEM((chunks, msgs, group, width), BF),
             pltpu.VMEM((2, hidden, width), BF),
             pltpu.VMEM((hidden, width), BF),
-            pltpu.VMEM((chunks, planes, part_rows, 2 * hidden), BF),
-            pltpu.VMEM((chunks, planes, part_rows, 2 * hidden), F32),
-            pltpu.VMEM((chunks, planes, part_rows, 2 * hidden), BF),
+            pltpu.VMEM((chunks, 2, planes, part_rows, hidden), BF),
+            pltpu.VMEM((chunks, 2, planes, part_rows, hidden), F32),
+            pltpu.VMEM((chunks, 2, 2, part_rows, hidden), BF),
+            pltpu.VMEM((chunks, 2, part_rows, hidden), BF),
+            pltpu.VMEM((chunks, 2, part_rows, hidden), BF),
             pltpu.VMEM((chunks, planes, part_rows, hidden), BF),
             pltpu.VMEM((chunks, msgs, group, width), BF),
             pltpu.VMEM((chunks, msgs, group, width), BF),
@@ -354,7 +384,8 @@
         + [dma((2, planes))] * 2
         + [dma((ring,))] * 2
         + [dma((chunks, msgs))] * 2
-        + [dma((chunks, planes))] * 4
+        + [dma((chunks, 2, 2))] * 2
+        + [dma((chunks, 2))] * 6
         + [dma((chunks, msgs))] * 2
         + [dma((ring,))] * 2
         + [dma((planes,))] * 2

time: 143 us -> 130 us (0.909)
  the two profiles are of different devices: /device:TPU:4 before, /device:TPU:1 now
where the time goes in v3:
time: 130 us; the launch traced here: 129 us
  Pallas kernels  128 us (98%)
  local copies, waits for them, and re-layouts  1.57 us (1%)
    pallas_call x1, Pallas kernels, on_device(): pl.pallas_call(functools.partial(kernel, (planes, ring, block, top, width...  128 us

profile of v3, /device:TPU:1, one launch (start us, length us, event | category | flops | bytes accessed | tf_op | source)
XLA Modules:
  0.0 129.4 jit_solution(327912995561210699)
XLA Ops:
  0.0 127.8 %shard_map.64 = bf16[16,4096]{1,0:T(8,128)(2,1)} custom-call(bf16[16,4096]{1,0:T(8,128)(2,1)} %tok_ref.1, s32[8,16]{1,0:T(8,128)} %bitcast.2, f32[8,16]{1,0:T(8,128)} %bitcast.3, bf16[1,192,4096]{2,1,0:T(8,128)(2,1)} %gate_ref.1, bf16[1,192,4096]{2,1,0:T(8,128)(2,1)} %up_ref.1, bf16[1,768,1024]{2,1,0:T(8,128)(2,1)} %down_ref.1), custom_call_target="tpu_custom_call" | custom-call | tf_op jit(solution)/shard_map/pallas_call | solution.py:356
  127.8 1.6 %copy.8 = bf16[16,4096]{1,0:T(8,128)(2,1)} copy(bf16[16,4096]{1,0:T(8,128)(2,1)} %shard_map.64) | data formatting | bytes 262144

commit v4 on v3

--- a/solution.py
+++ b/solution.py
@@ -56,6 +56,9 @@
             device_id=device, device_id_type=MESH,
         )
 
+    def wait_in(buf, sem):
+        pltpu.make_async_copy(buf, buf, sem).wait()
+
     def col(p):
         return pl.ds(pl.multiple_of(p * width, 128), width)
 
@@ -113,10 +116,25 @@
         for cp in x_copies(step):
             cp.wait_recv()
 
+    reach = ring // 4 or ring
+    direct = [i for i in range(1, ring) if min(order[i], ring - order[i]) <= reach]
+    relays = [(sign, e) for sign in (1, -1) for e in range(1, reach + 1) if reach < ring]
+    opposite = order.index(ring // 2)
+
     def ag_copy(i):
         return remote(rows_all.at[0], rows_all.at[back[i]], s_ag.at[i], r_ag.at[back[i]], along(order[i], 1 - c, c))
 
-    for i in range(1, ring):
+    def on_copy(sign, e):
+        source, there = order.index(-sign * reach % ring), order.index(-sign * (reach + e) % ring)
+        part = pl.ds(0, rows)
+        if there == opposite:
+            part = pl.ds(0 if sign > 0 else rows // 2, rows // 2)
+        return remote(
+            rows_all.at[source, part, :], rows_all.at[there, part, :], s_ag.at[ring + relays.index((sign, e))],
+            r_ag.at[ring if there == opposite and sign < 0 else there], along(sign * e % ring, 1 - c, c),
+        )
+
+    for i in direct:
         ag_copy(i).start()
 
     def w_copies(step):
@@ -158,8 +176,12 @@
 
     def place(k):
         for i in (2 * k, 2 * k + 1):
-            if i:
-                remote(rows_all.at[0], rows_all.at[i], s_ag.at[i], r_ag.at[i], x_peer(1)).wait_recv()
+            if i and i not in direct:
+                if i == opposite:
+                    wait_in(rows_all.at[i, pl.ds(0, rows // 2), :], r_ag.at[i])
+                    wait_in(rows_all.at[i, pl.ds(rows // 2, rows // 2), :], r_ag.at[ring])
+                else:
+                    wait_in(rows_all.at[i], r_ag.at[i])
         both = rows_all[2 * k:2 * k + 2].reshape(2 * rows, width + META)
         meta = both[:, width:].astype(F32)
         hits = jnp.zeros(shape, F32)
@@ -183,9 +205,6 @@
                     a_copy(k, i, dc).start()
         own_slots(k).start()
 
-    def wait_in(buf, sem):
-        pltpu.make_async_copy(buf, buf, sem).wait()
-
     near = (r + 1 - 2 * (r % 2), planes - 1 - r)
     far = (r + 2) % planes
 
@@ -219,6 +238,10 @@
                 p_copy(k, half, n).start()
 
     def pass_on(k):
+        for i in range(ring):
+            for dc in range(2):
+                if i or dc:
+                    a_copy(k, i, dc).wait_send()
         for half in range(2):
             p_copy(k, half, 1).wait_recv()
             fwd[k, half] = (pown[k, half, near[1 - half]] + precv[k, half, 1].astype(F32)).astype(BF)
@@ -269,7 +292,24 @@
     def z_copy(i):
         return remote(zsend.at[i], zrecv.at[back[i]], s_z.at[i], r_z.at[back[i]], along(order[i], 1 - c, c))
 
+    def back_sent(k):
+        for m in range(msgs):
+            if m < 2:
+                @pl.when(c != m)
+                def _():
+                    b_copy(k, m).wait_send()
+            else:
+                b_copy(k, m).wait_send()
+
     def mix(k):
+        for n in range(2):
+            p_copy(k, n, 0).wait_send()
+            p_copy(k, n, 1).wait_send()
+            q_copy(k, n).wait_send()
+            h_copy(k, n).wait_send()
+            g_copy(k, n).wait_send()
+        if k != turns[0]:
+            back_sent(turns[turns.index(k) - 1])
         for jj in range(msgs):
             wait_in(returned.at[k, jj], r_b.at[k, jj])
         got = returned[k].reshape(lanes, width)
@@ -280,7 +320,12 @@
             if i:
                 z_copy(i).start()
 
-    for k in range(chunks):
+    turns = [*range(1, chunks), 0]
+    for i in direct:
+        wait_in(rows_all.at[i], r_ag.at[i])
+    for sign, e in relays:
+        on_copy(sign, e).start()
+    for k in turns:
         place(k)
     for cp in own[1:]:
         cp.wait()
@@ -288,8 +333,8 @@
         for cp in w_copies(step):
             cp.wait_recv()
     stages = []
-    for n, k in enumerate([*range(1, chunks), 0]):
-        for depth, (late, stage) in enumerate(((0, first), (4, pass_on), (7, second), (10, relay), (13, third), (17, mix))):
+    for n, k in enumerate(turns):
+        for depth, (late, stage) in enumerate(((-30 - 2 * n, first), (10, pass_on), (14, second), (18, relay), (22, third), (29, mix))):
             stages.append((3 * n + late, -depth, stage, k))
     for _, _, stage, k in sorted(stages, key=lambda e: e[:2]):
         stage(k)
@@ -312,27 +357,13 @@
     for step in range(1, planes):
         for cp in x_copies(step) + w_copies(step):
             cp.wait_send()
+    for i in direct:
+        ag_copy(i).wait_send()
+    for sign, e in relays:
+        on_copy(sign, e).wait_send()
     for i in range(1, ring):
-        ag_copy(i).wait_send()
         z_copy(i).wait_send()
-    for k in range(chunks):
-        for n in range(2):
-            p_copy(k, n, 0).wait_send()
-            p_copy(k, n, 1).wait_send()
-            q_copy(k, n).wait_send()
-            h_copy(k, n).wait_send()
-            g_copy(k, n).wait_send()
-        for i in range(ring):
-            for dc in range(2):
-                if i or dc:
-                    a_copy(k, i, dc).wait_send()
-        for m in range(msgs):
-            if m < 2:
-                @pl.when(c != m)
-                def _():
-                    b_copy(k, m).wait_send()
-            else:
-                b_copy(k, m).wait_send()
+    back_sent(turns[-1])
 
     own_cols.wait()
     for step in range(1, planes):
@@ -382,7 +413,7 @@
         ]
         + [dma((planes,))] * 4
         + [dma((2, planes))] * 2
-        + [dma((ring,))] * 2
+        + [dma((2 * ring,)), dma((ring + 1,))]
         + [dma((chunks, msgs))] * 2
         + [dma((chunks, 2, 2))] * 2
         + [dma((chunks, 2))] * 6

time: 130 us -> 134 us (1.031)
  Pallas kernels: 128 us -> 131 us
    pallas_call x1, Pallas kernels: 128 us -> 131 us  [on_device(): pl.pallas_call(functools.partial(kernel, (planes, ring, block, top, width...]
where the time goes in v4:
time: 134 us; the launch traced here: 133 us
  Pallas kernels  131 us (98%)
  local copies, waits for them, and re-layouts  1.57 us (1%)
    pallas_call x1, Pallas kernels, on_device(): pl.pallas_call(functools.partial(kernel, (planes, ring, block, top, width...  131 us

profile of v4, /device:TPU:1, one launch (start us, length us, event | category | flops | bytes accessed | tf_op | source)
XLA Modules:
  0.0 133.0 jit_solution(14763371028329943621)
XLA Ops:
  0.0 131.4 %shard_map.64 = bf16[16,4096]{1,0:T(8,128)(2,1)} custom-call(bf16[16,4096]{1,0:T(8,128)(2,1)} %tok_ref.1, s32[8,16]{1,0:T(8,128)} %bitcast.2, f32[8,16]{1,0:T(8,128)} %bitcast.3, bf16[1,192,4096]{2,1,0:T(8,128)(2,1)} %gate_ref.1, bf16[1,192,4096]{2,1,0:T(8,128)(2,1)} %up_ref.1, bf16[1,768,1024]{2,1,0:T(8,128)(2,1)} %down_ref.1), custom_call_target="tpu_custom_call" | custom-call | tf_op jit(solution)/shard_map/pallas_call | solution.py:387
  131.4 1.6 %copy.8 = bf16[16,4096]{1,0:T(8,128)(2,1)} copy(bf16[16,4096]{1,0:T(8,128)(2,1)} %shard_map.64) | data formatting | bytes 262144

commit v5 on v3

--- a/solution.py
+++ b/solution.py
@@ -23,7 +23,7 @@
     planes, ring, block, top, width, hidden = dims
     (
         meta_ref, rows_all, outgoing, arrived, weights, down, psend, pown, precv, fwd, frecv, hid, outs,
-        returned, mix_hi, mix_lo, zsend, zrecv, fin, cols,
+        returned, mix_hi, mix_lo, zsend, zrecv, fin, tsum,
         s_x, r_x, s_m, r_m, s_w, r_w, s_ag, r_ag, s_a, r_a, s_p, r_p, s_q, r_q, s_h, r_h, s_g, r_g,
         s_b, r_b, s_z, r_z, s_f, r_f, l_sem,
     ) = scratch
@@ -269,7 +269,15 @@
     def z_copy(i):
         return remote(zsend.at[i], zrecv.at[back[i]], s_z.at[i], r_z.at[back[i]], along(order[i], 1 - c, c))
 
+    early = [i for i in range(1, ring) if 1 <= back[i] // 2 < chunks - 1]
+
     def mix(k):
+        if k == 0:
+            total = jnp.zeros((rows, width), F32)
+            for i in early:
+                wait_in(zrecv.at[i], r_z.at[i])
+                total = total + zrecv[i].astype(F32)
+            tsum[...] = total
         for jj in range(msgs):
             wait_in(returned.at[k, jj], r_b.at[k, jj])
         got = returned[k].reshape(lanes, width)
@@ -294,19 +302,19 @@
     for _, _, stage, k in sorted(stages, key=lambda e: e[:2]):
         stage(k)
 
-    total = zsend[0].astype(F32)
-    for i in range(1, ring):
+    total = tsum[...] + zsend[0].astype(F32)
+    for i in (i for i in range(1, ring) if i not in early):
         wait_in(zrecv.at[i], r_z.at[i])
         total = total + zrecv[i].astype(F32)
     fin[...] = total.astype(BF).reshape(planes, block, width)
 
     def f_copy(step):
         p = (r + step) % planes
-        return remote(fin.at[p], cols.at[r], s_f.at[step], r_f.at[step], x_peer(step))
+        return remote(fin.at[p], out_ref.at[:, col(r)], s_f.at[step], r_f.at[step], x_peer(step))
 
     for step in range(1, planes):
         f_copy(step).start()
-    own_cols = pltpu.make_async_copy(fin.at[r], cols.at[r], l_sem.at[5])
+    own_cols = pltpu.make_async_copy(fin.at[r], out_ref.at[:, col(r)], l_sem.at[5])
     own_cols.start()
 
     for step in range(1, planes):
@@ -336,9 +344,7 @@
 
     own_cols.wait()
     for step in range(1, planes):
-        wait_in(cols.at[(r + planes - step) % planes], r_f.at[step])
-    for p in range(planes):
-        out_ref[:, p * width:(p + 1) * width] = cols[p]
+        wait_in(out_ref.at[:, col((r + planes - step) % planes)], r_f.at[step])
     for step in range(1, planes):
         f_copy(step).wait_send()
 
@@ -357,7 +363,7 @@
         functools.partial(kernel, (planes, ring, block, top, width, hidden)),
         out_shape=jax.ShapeDtypeStruct(tokens.shape, BF),
         in_specs=[pl.BlockSpec(memory_space=pltpu.VMEM)] * 3 + [pl.BlockSpec(memory_space=pl.ANY)] * 3,
-        out_specs=pl.BlockSpec(memory_space=pltpu.VMEM),
+        out_specs=pl.BlockSpec(memory_space=pl.ANY),
         scratch_shapes=[
             pltpu.VMEM((block, META), BF),
             pltpu.VMEM((ring, rows, width + META), BF),
@@ -378,7 +384,7 @@
             pltpu.VMEM((ring, rows, width), BF),
             pltpu.VMEM((ring, rows, width), BF),
             pltpu.VMEM((planes, block, width), BF),
-            pltpu.VMEM((planes, block, width), BF),
+            pltpu.VMEM((rows, width), F32),
         ]
         + [dma((planes,))] * 4
         + [dma((2, planes))] * 2

time: 130 us -> 130 us (level)
  no operation moved by 1% of the time
where the time goes in v5:
time: 130 us; the launch traced here: 129 us
  Pallas kernels  127 us (98%)
  local copies, waits for them, and re-layouts  1.57 us (1%)
    pallas_call x1, Pallas kernels, on_device(): pl.pallas_call(functools.partial(kernel, (planes, ring, block, top, width...  127 us

profile of v5, /device:TPU:1, one launch (start us, length us, event | category | flops | bytes accessed | tf_op | source)
XLA Modules:
  0.0 128.7 jit_solution(7933351823636894902)
XLA Ops:
  0.0 127.2 %shard_map.64 = bf16[16,4096]{1,0:T(8,128)(2,1)} custom-call(bf16[16,4096]{1,0:T(8,128)(2,1)} %tok_ref.1, s32[8,16]{1,0:T(8,128)} %bitcast.2, f32[8,16]{1,0:T(8,128)} %bitcast.3, bf16[1,192,4096]{2,1,0:T(8,128)(2,1)} %gate_ref.1, bf16[1,192,4096]{2,1,0:T(8,128)(2,1)} %up_ref.1, bf16[1,768,1024]{2,1,0:T(8,128)(2,1)} %down_ref.1), custom_call_target="tpu_custom_call" | custom-call | tf_op jit(solution)/shard_map/pallas_call | solution.py:362
  127.2 1.6 %copy.8 = bf16[16,4096]{1,0:T(8,128)(2,1)} copy(bf16[16,4096]{1,0:T(8,128)(2,1)} %shard_map.64) | data formatting | bytes 262144
